TPU v7x, 256 devices: a whole 4x4x8 slice. The times are simulated.
256 devices in a mesh: seq: 16 (over y_lo, x, core), tp: 16 (over z, y_hi).
Axes of the slice: x: 4, y: 4 (y_hi: 2, y_lo: 2; y = y_hi * 2 + y_lo), z: 8, core: 2. Of those that a mesh axis runs over, the one named last changes fastest.
Arguments:
- tokens: bfloat16 [4096, 5376], P('seq', 'tp'), may hold values from -24 to 24
- w_query: bfloat16 [5376, 4096], P('seq', 'tp'), may hold values from -0.078125 to 0.078125
- w_key: bfloat16 [5376, 2048], P('seq', 'tp'), may hold values from -0.078125 to 0.078125
- w_value: bfloat16 [5376, 2048], P('seq', 'tp'), may hold values from -0.078125 to 0.078125
- w_out: bfloat16 [4096, 5376], P('tp', 'seq'), may hold values from -0.09375 to 0.09375
- cotangent: bfloat16 [4096, 5376], P('seq', 'tp'), may hold values from -6 to 6
- block_lists: int32 [32, 9], P('seq'), may hold values from -1 to 31, as said below
Outputs:
- grad_tokens: bfloat16 [4096, 5376], P('seq', 'tp')
- grad_query: bfloat16 [5376, 4096], P('seq', 'tp')
- grad_key: bfloat16 [5376, 2048], P('seq', 'tp')
- grad_value: bfloat16 [5376, 2048], P('seq', 'tp')
- grad_w_out: bfloat16 [4096, 5376], P('tp', 'seq')
Inputs may be any that keep to these rules, and one draw needn't show every extreme that they name: `block_lists`: entry k of query block b is b - 8 + k if that key block lies in the same document as block b, else -1. Documents are runs of whole blocks; the last entry of each row is b, and the valid entries of a row are its last ones.
All inputs are finite; a program needn't handle non-finite values.
Results may differ from a plain program's by a relative error of at most 0.025.
Values may be sent and summed in bfloat16 or wider, within the bound.
No kernel may reach another device: no remote copies, remote signals or barrier semaphores. Data moves between devices by JAX's collectives and lax.ppermute only.
A program may use at most 64 MiB of HBM per device.

v0:
```python
import jax
import jax.numpy as jnp
from jax import lax
from jax.sharding import PartitionSpec as P

HEADS = 32
KV_HEADS = 16
HD = 128
WIN = 1024
ATTN_SCALAR = 168


def from_behind(block, axis, distance):
    devices = range(lax.axis_size(axis))
    route = [(i - distance, i) for i in devices if i - distance in devices]
    return lax.ppermute(block, axis, route)


def window_view(blocks, n_blocks, span):
    return jnp.concatenate([blocks[offset : offset + n_blocks] for offset in range(span)], axis=1)


def fold_windows(windows, n_blocks, span, block_len):
    shaped = windows.reshape(n_blocks, span, block_len, windows.shape[2], windows.shape[3])
    summed = jnp.zeros(
        (n_blocks + span - 1, block_len, windows.shape[2], windows.shape[3]), jnp.float32
    )
    for offset in range(span):
        summed = summed.at[offset : offset + n_blocks].add(shaped[:, offset])
    return summed.reshape((n_blocks + span - 1) * block_len, windows.shape[2] * windows.shape[3])


def local_attention(query, keys, values, d_attn, block_lists, softmax_scale):
    tok_rows, kv_local, group_size, head_dim = query.shape
    n_blocks, span = block_lists.shape
    block_len = tok_rows // n_blocks
    width = span * block_len
    key_blocks = keys.reshape(n_blocks + span - 1, block_len, kv_local, head_dim)
    val_blocks = values.reshape(n_blocks + span - 1, block_len, kv_local, head_dim)
    key_win = window_view(key_blocks, n_blocks, span)
    val_win = window_view(val_blocks, n_blocks, span)
    q_blocks = query.reshape(n_blocks, block_len, kv_local, group_size, head_dim)
    grad_blocks = d_attn.reshape(n_blocks, block_len, kv_local, group_size, head_dim)
    scores = (
        jnp.einsum("btkgd,bwkd->bkgtw", q_blocks, key_win, preferred_element_type=jnp.float32)
        * softmax_scale
    )
    rows_at = jnp.arange(block_len)[:, None]
    cols_at = jnp.arange(width)[None, :]
    inside = (cols_at > rows_at) & (cols_at <= rows_at + (width - block_len))
    listed = jnp.repeat(block_lists >= 0, block_len, axis=1)
    allowed = inside[None, None, None] & listed[:, None, None, None, :]
    masked = jnp.where(allowed, scores, -1e30)
    highest = jnp.max(masked, axis=-1, keepdims=True)
    weights = jnp.where(allowed, jnp.exp(masked - highest), 0.0)
    probs = weights / jnp.sum(weights, axis=-1, keepdims=True)
    probs_half = probs.astype(jnp.bfloat16)
    attn = jnp.einsum(
        "bkgtw,bwkd->btkgd", probs_half, val_win, preferred_element_type=jnp.float32
    ).astype(jnp.bfloat16)
    delta = jnp.sum(grad_blocks.astype(jnp.float32) * attn.astype(jnp.float32), axis=-1)
    delta = jnp.transpose(delta, (0, 2, 3, 1))[..., None]
    grad_probs = jnp.einsum(
        "btkgd,bwkd->bkgtw", grad_blocks, val_win, preferred_element_type=jnp.float32
    )
    grad_scores = (probs * (grad_probs - delta)).astype(jnp.bfloat16)
    grad_q = (
        jnp.einsum("bkgtw,bwkd->btkgd", grad_scores, key_win, preferred_element_type=jnp.float32)
        * softmax_scale
    ).astype(jnp.bfloat16)
    grad_kwin = (
        jnp.einsum("bkgtw,btkgd->bwkd", grad_scores, q_blocks, preferred_element_type=jnp.float32)
        * softmax_scale
    )
    grad_vwin = jnp.einsum(
        "bkgtw,btkgd->bwkd", probs_half, grad_blocks, preferred_element_type=jnp.float32
    )
    grad_keys = fold_windows(grad_kwin, n_blocks, span, block_len)
    grad_values = fold_windows(grad_vwin, n_blocks, span, block_len)
    flat = kv_local * group_size * head_dim
    return (attn.reshape(tok_rows, flat), grad_q.reshape(tok_rows, flat), grad_keys, grad_values)


def contract_cols(left, right):
    return lax.dot_general(
        left, right, (((1,), (1,)), ((), ())), preferred_element_type=jnp.float32
    )


def term_maker(left, right):
    return lax.dot_general(
        left, right, (((0,), (0,)), ((), ())), preferred_element_type=jnp.float32
    )


def shards(tokens, w_query, w_key, w_value, w_out, cotangent, block_lists):
    softmax_scale = ATTN_SCALAR ** (-0.5)
    group_size = HEADS // KV_HEADS
    head_dim = HD
    tok_rows = tokens.shape[0]
    reach = WIN // tok_rows
    full_tokens, full_cot = (
        lax.all_gather(tokens, "tp", axis=1, tiled=True),
        lax.all_gather(cotangent, "tp", axis=1, tiled=True),
    )
    query_full, key_full, value_full = (
        lax.all_gather(w_query, "seq", axis=0, tiled=True),
        lax.all_gather(w_key, "seq", axis=0, tiled=True),
        lax.all_gather(w_value, "seq", axis=0, tiled=True),
    )
    d_attn = contract_cols(full_cot, lax.all_gather(w_out, "seq", axis=1, tiled=True)).astype(
        jnp.bfloat16
    )
    query = jnp.dot(full_tokens, query_full, preferred_element_type=jnp.float32).astype(
        jnp.bfloat16
    )
    keys = jnp.dot(full_tokens, key_full, preferred_element_type=jnp.float32).astype(jnp.bfloat16)
    values = jnp.dot(full_tokens, value_full, preferred_element_type=jnp.float32).astype(
        jnp.bfloat16
    )
    earlier = [from_behind((keys, values), "seq", distance) for distance in range(reach, 0, -1)]
    key_ext = jnp.concatenate([member[0] for member in earlier] + [keys], axis=0)
    value_ext = jnp.concatenate([member[1] for member in earlier] + [values], axis=0)
    kv_local = keys.shape[1] // head_dim
    attn, grad_q, grad_k_ext, grad_v_ext = local_attention(
        query.reshape(tok_rows, kv_local, group_size, head_dim),
        key_ext.reshape(-1, kv_local, head_dim),
        value_ext.reshape(-1, kv_local, head_dim),
        d_attn.reshape(tok_rows, kv_local, group_size, head_dim),
        block_lists,
        softmax_scale,
    )

    def segment(array, index):
        return array[index * tok_rows : (index + 1) * tok_rows]

    summed_k = segment(grad_k_ext, reach)
    summed_v = segment(grad_v_ext, reach)
    for distance in range(1, reach + 1):
        back_k, back_v = from_behind(
            (segment(grad_k_ext, reach - distance), segment(grad_v_ext, reach - distance)),
            "seq",
            -distance,
        )
        summed_k = summed_k + back_k
        summed_v = summed_v + back_v
    grad_k = summed_k.astype(jnp.bfloat16)
    grad_v = summed_v.astype(jnp.bfloat16)
    token_term = (
        contract_cols(grad_q, query_full)
        + contract_cols(grad_k, key_full)
        + contract_cols(grad_v, value_full)
    )
    grad_tokens = lax.psum_scatter(token_term, "tp", scatter_dimension=1, tiled=True).astype(
        jnp.bfloat16
    )
    operand_pairs = (
        (full_tokens, grad_q),
        (full_tokens, grad_k),
        (full_tokens, grad_v),
        (full_cot, attn),
    )

    def reduce_rows(left, right):
        return lax.psum_scatter(
            term_maker(left, right).astype(jnp.bfloat16), "seq", scatter_dimension=0, tiled=True
        ).astype(jnp.float32)

    results = [reduce_rows(left, right) for left, right in operand_pairs]
    grad_query = results[0].astype(jnp.bfloat16)
    grad_key = results[1].astype(jnp.bfloat16)
    grad_value = results[2].astype(jnp.bfloat16)
    grad_w_out = results[3].T.astype(jnp.bfloat16)
    return (grad_tokens, grad_query, grad_key, grad_value, grad_w_out)


def solution(mesh):
    in_specs = (
        P("seq", "tp"),
        P("seq", "tp"),
        P("seq", "tp"),
        P("seq", "tp"),
        P("tp", "seq"),
        P("seq", "tp"),
        P("seq", None),
    )
    out_specs = (P("seq", "tp"), P("seq", "tp"), P("seq", "tp"), P("seq", "tp"), P("tp", "seq"))
    return jax.shard_map(shards, mesh=mesh, in_specs=in_specs, out_specs=out_specs, check_vma=False)
```

profile of v0, /device:TPU:32, one launch (start us, length us, event | category | flops | bytes accessed | tf_op | source)
XLA Modules:
  0.0 933.3 jit_solution(3593583309488818795)
XLA Ops:
  12.6 35.0 %all-gather.9.cloned.1.call-done = bf16[5376,128]{1,0:T(8,128)(2,1)} async-done(((bf16[336,128]{1,0:T(8,128)(2,1)}), bf16[5376,128]{1,0:T(8,128)(2,1)}) %all-gather.9.cloned.1.call-update) | async-done | bytes 1376272 | tf_op jit(solution)/shard_map/all_gather | solution.py:108
  47.6 92.1 %all-gather.7.cloned.1.call-done = bf16[256,5376]{0,1:T(8,128)(2,1)} async-done(((bf16[256,336]{0,1:T(8,128)(2,1)}), bf16[256,5376]{0,1:T(8,128)(2,1)}) %all-gather.7.cloned.1.call-update) | async-done | bytes 2752528 | tf_op jit(solution)/shard_map/all_gather | solution.py:103
  139.7 3.2 convolution_convert_fusion.7
  143.0 5.5 collective-permute-start
  148.5 1.9 collective-permute-start.1
  150.4 3.1 collective-permute-start.2
  153.4 3.3 collective-permute-start.3
  156.7 20.5 %all-gather.11.cloned.1.call-done = bf16[5376,256]{1,0:T(8,128)(2,1)} async-done(((bf16[336,256]{1,0:T(8,128)(2,1)}), bf16[5376,256]{1,0:T(8,128)(2,1)}) %all-gather.11.cloned.1.call-update) | async-done | bytes 2752528 | tf_op jit(solution)/shard_map/all_gather | solution.py:107
  177.2 3.4 convolution_convert_fusion.5
  180.6 87.6 %all-gather.15.cloned.1.call-done = bf16[256,5376]{0,1:T(8,128)(2,1)} async-done(((bf16[256,336]{0,1:T(8,128)(2,1)}), bf16[256,5376]{0,1:T(8,128)(2,1)}) %all-gather.15.cloned.1.call-update) | async-done | bytes 2752528 | tf_op jit(solution)/shard_map/all_gather | solution.py:104
  268.2 36.3 %all-gather.17.cloned.1.call-done = bf16[256,5376]{0,1:T(8,128)(2,1)} async-done(((bf16[256,336]{0,1:T(8,128)(2,1)}), bf16[256,5376]{0,1:T(8,128)(2,1)}) %all-gather.17.cloned.1.call-update) | async-done | bytes 2752528 | tf_op jit(solution)/shard_map/all_gather | solution.py:111
  304.5 3.5 convolution_convert_fusion.4
  308.0 33.5 %all-gather.13.cloned.1.call-done = bf16[5376,128]{1,0:T(8,128)(2,1)} async-done(((bf16[336,128]{1,0:T(8,128)(2,1)}), bf16[5376,128]{1,0:T(8,128)(2,1)}) %all-gather.13.cloned.1.call-update) | async-done | bytes 1376272 | tf_op jit(solution)/shard_map/all_gather | solution.py:109
  341.5 2.3 convolution_convert_fusion.6
  344.5 1.0 reshape.830
  345.5 1.6 reshape.805
  347.1 1.7 copy.86
  348.8 1.7 copy.97
  350.5 4.0 collective-permute-start.4
  355.3 2.0 collective-permute-start.5
  358.2 3.5 collective-permute-start.6
  361.6 3.0 collective-permute-start.7
  368.2 1.4 fusion.79
  370.1 1.8 convolution_bitcast_fusion.1
  373.8 1.5 fusion.11
  375.7 2.7 copy.99
  380.3 0.9 fusion.53
  381.3 0.9 fusion.51
  382.2 0.9 fusion.49
  383.2 0.9 fusion.47
  384.1 0.9 fusion.45
  386.0 1.7 fusion.41
  387.7 1.3 collective-permute-start.12
  389.0 2.7 copy.88
  396.4 0.9 fusion.60
  399.3 1.7 fusion.54
  401.0 1.3 collective-permute-start.10
  402.3 1.3 collective-permute-start.11
  403.6 1.3 collective-permute-start.8
  404.9 1.5 collective-permute-start.9
  406.5 2.8 fusion.39
  409.4 1.3 collective-permute-start.13
  410.7 2.9 collective-permute-done.11
  413.6 1.3 collective-permute-start.14
  414.9 1.3 collective-permute-start.15
  416.2 1.1 fusion.74
  418.3 1.4 collective-permute-done.13
  419.6 1.4 collective-permute-done.14
  421.0 5.3 collective-permute-done.15
  426.4 3.3 convolution_add_fusion
  429.7 2.2 fusion.3
  431.9 2.5 copy.131
  434.5 2.2 fusion.2
  436.7 2.5 copy.129
  439.2 2.6 fusion
  441.8 4.5 copy.127
  446.6 2.8 fusion.1
  449.4 2.9 copy.133
  452.3 201.1 %reduce-scatter.14.cloned.1.call-done = f32[256,336]{0,1:T(8,128)} async-done(((f32[256,5376]{0,1:T(8,128)}), f32[256,336]{0,1:T(8,128)}) %reduce-scatter.14.cloned.1.call-update) | async-done | bytes 344080 | tf_op jit(solution)/shard_map/reduce_scatter | solution.py:154
  653.4 1.7 convert_element_type.114
  655.1 65.9 %reduce-scatter.20.cloned.1.call-done = bf16[336,128]{1,0:T(8,128)(2,1)} async-done(((bf16[5376,128]{1,0:T(8,128)(2,1)}), bf16[336,128]{1,0:T(8,128)(2,1)}) %reduce-scatter.20.cloned.1.call-update) | async-done | bytes 86032
  721.0 67.3 %reduce-scatter.18.cloned.1.call-done = bf16[336,128]{1,0:T(8,128)(2,1)} async-done(((bf16[5376,128]{1,0:T(8,128)(2,1)}), bf16[336,128]{1,0:T(8,128)(2,1)}) %reduce-scatter.18.cloned.1.call-update) | async-done | bytes 86032
  788.2 69.2 %reduce-scatter.16.cloned.1.call-done = bf16[336,256]{1,0:T(8,128)(2,1)} async-done(((bf16[5376,256]{1,0:T(8,128)(2,1)}), bf16[336,256]{1,0:T(8,128)(2,1)}) %reduce-scatter.16.cloned.1.call-update) | async-done | bytes 172048
  857.4 69.3 %reduce-scatter.22.cloned.1.call-done = bf16[336,256]{1,0:T(8,128)(2,1)} async-done(((bf16[5376,256]{1,0:T(8,128)(2,1)}), bf16[336,256]{1,0:T(8,128)(2,1)}) %reduce-scatter.22.cloned.1.call-update) | async-done | bytes 172048
  (102 shorter events, 24.8 us)
Async XLA Ops:
  7.2 40.4 %all-gather.9.cloned.1.call-start = ((), (), s32[]{:S(2)}) async-start(), calls=%async_computation.6 | async-start | bytes 1462272 | tf_op jit(solution)/shard_map/all_gather | solution.py:108
  7.9 131.8 %all-gather.7.cloned.1.call-start = ((), (), s32[]{:S(2)}) async-start(), calls=%async_computation.5 | async-start | bytes 2924544 | tf_op jit(solution)/shard_map/all_gather | solution.py:103
  8.6 168.6 %all-gather.11.cloned.1.call-start = ((), (), s32[]{:S(2)}) async-start(), calls=%async_computation.7 | async-start | bytes 2924544 | tf_op jit(solution)/shard_map/all_gather | solution.py:107
  9.4 258.8 %all-gather.15.cloned.1.call-start = ((), (), s32[]{:S(2)}) async-start(), calls=%async_computation.9 | async-start | bytes 2924544 | tf_op jit(solution)/shard_map/all_gather | solution.py:104
  10.0 294.5 %all-gather.17.cloned.1.call-start = ((), (), s32[]{:S(2)}) async-start(), calls=%async_computation.10 | async-start | bytes 2924544 | tf_op jit(solution)/shard_map/all_gather | solution.py:111
  10.5 331.0 %all-gather.13.cloned.1.call-start = ((), (), s32[]{:S(2)}) async-start(), calls=%async_computation.8 | async-start | bytes 1462272 | tf_op jit(solution)/shard_map/all_gather | solution.py:109
  11.1 642.3 %reduce-scatter.14.cloned.1.call-start = ((), (), s32[]{:S(2)}) async-start(), calls=%async_computation.11 | async-start | bytes 5849088 | tf_op jit(solution)/shard_map/reduce_scatter | solution.py:154
  139.7 37.5 %copy-start = (bf16[256,5376]{0,1:T(8,128)(2,1)S(1)}, bf16[256,5376]{0,1:T(8,128)(2,1)}, u32[]{:S(2)}) copy-start(bf16[256,5376]{0,1:T(8,128)(2,1)} %all-gather.7.cloned.1.call-done) | copy-start | bytes 8257540
  143.0 212.3 %collective-permute-start = (bf16[256,128]{1,0:T(8,128)(2,1)S(1)}, bf16[256,128]{1,0:T(8,128)(2,1)}, u32[]{:S(2)}, u32[]{:S(2)}) collective-permute-start(bf16[256,128]{1,0:T(8,128)(2,1)S(1)} %convolution_convert_fusion.7), channel_id=1, source_target_pairs={{0,64},{16,80},{32,96},{48,112},{64,128},{80,144},{96,160},{112,17... | collective-permute-start | bytes 196616 | tf_op jit(solution)/shard_map/ppermute | solution.py:16
  148.5 209.7 %collective-permute-start.1 = (bf16[256,128]{1,0:T(8,128)(2,1)S(1)}, bf16[256,128]{1,0:T(8,128)(2,1)}, u32[]{:S(2)}, u32[]{:S(2)}) collective-permute-start(bf16[256,128]{1,0:T(8,128)(2,1)S(1)} %convolution_convert_fusion.7), channel_id=1, source_target_pairs={{0,48},{16,64},{32,80},{48,96},{64,112},{80,128},{96,144},{112,160... | collective-permute-start | bytes 196616 | tf_op jit(solution)/shard_map/ppermute | solution.py:16
  150.4 211.3 %collective-permute-start.2 = (bf16[256,128]{1,0:T(8,128)(2,1)S(1)}, bf16[256,128]{1,0:T(8,128)(2,1)}, u32[]{:S(2)}, u32[]{:S(2)}) collective-permute-start(bf16[256,128]{1,0:T(8,128)(2,1)S(1)} %convolution_convert_fusion.7), channel_id=1, source_target_pairs={{0,32},{16,48},{32,64},{48,80},{64,96},{80,112},{96,128},{112,144}... | collective-permute-start | bytes 196616 | tf_op jit(solution)/shard_map/ppermute | solution.py:16
  153.4 211.2 %collective-permute-start.3 = (bf16[256,128]{1,0:T(8,128)(2,1)S(1)}, bf16[256,128]{1,0:T(8,128)(2,1)}, u32[]{:S(2)}, u32[]{:S(2)}) collective-permute-start(bf16[256,128]{1,0:T(8,128)(2,1)S(1)} %convolution_convert_fusion.7), channel_id=1, source_target_pairs={{0,16},{16,32},{32,48},{48,64},{64,80},{80,96},{96,112},{112,128},... | collective-permute-start | bytes 196616 | tf_op jit(solution)/shard_map/ppermute | solution.py:16
  308.0 35.8 %copy-start.4 = (bf16[256,256]{1,0:T(8,128)(2,1)}, bf16[256,256]{1,0:T(8,128)(2,1)S(1)}, u32[]{:S(2)}) copy-start(bf16[256,256]{1,0:T(8,128)(2,1)S(1)} %convolution_convert_fusion.4) | copy-start | bytes 393220
  350.5 21.4 %collective-permute-start.4 = (bf16[256,128]{1,0:T(8,128)(2,1)S(1)}, bf16[256,128]{1,0:T(8,128)(2,1)S(1)}, u32[]{:S(2)}, u32[]{:S(2)}) collective-permute-start(bf16[256,128]{1,0:T(8,128)(2,1)S(1)} %convolution_convert_fusion.6), channel_id=1, source_target_pairs={{0,64},{16,80},{32,96},{48,112},{64,128},{80,144},{96,160},{112,17... | collective-permute-start | bytes 196616 | tf_op jit(solution)/shard_map/ppermute | solution.py:16
  355.3 16.6 %collective-permute-start.5 = (bf16[256,128]{1,0:T(8,128)(2,1)S(1)}, bf16[256,128]{1,0:T(8,128)(2,1)S(1)}, u32[]{:S(2)}, u32[]{:S(2)}) collective-permute-start(bf16[256,128]{1,0:T(8,128)(2,1)S(1)} %convolution_convert_fusion.6), channel_id=1, source_target_pairs={{0,48},{16,64},{32,80},{48,96},{64,112},{80,128},{96,144},{112,160... | collective-permute-start | bytes 196616 | tf_op jit(solution)/shard_map/ppermute | solution.py:16
  358.2 13.8 %collective-permute-start.6 = (bf16[256,128]{1,0:T(8,128)(2,1)S(1)}, bf16[256,128]{1,0:T(8,128)(2,1)S(1)}, u32[]{:S(2)}, u32[]{:S(2)}) collective-permute-start(bf16[256,128]{1,0:T(8,128)(2,1)S(1)} %convolution_convert_fusion.6), channel_id=1, source_target_pairs={{0,32},{16,48},{32,64},{48,80},{64,96},{80,112},{96,128},{112,144}... | collective-permute-start | bytes 196616 | tf_op jit(solution)/shard_map/ppermute | solution.py:16
  361.6 10.3 %collective-permute-start.7 = (bf16[256,128]{1,0:T(8,128)(2,1)S(1)}, bf16[256,128]{1,0:T(8,128)(2,1)S(1)}, u32[]{:S(2)}, u32[]{:S(2)}) collective-permute-start(bf16[256,128]{1,0:T(8,128)(2,1)S(1)} %convolution_convert_fusion.6), channel_id=1, source_target_pairs={{0,16},{16,32},{32,48},{48,64},{64,80},{80,96},{96,112},{112,128},... | collective-permute-start | bytes 196616 | tf_op jit(solution)/shard_map/ppermute | solution.py:16
  368.2 1.9 copy-start.6
  370.1 2.0 copy-start.5
  372.9 0.9 copy-start.3
  387.7 30.5 %collective-permute-start.12 = (f32[256,128]{1,0:T(8,128)}, f32[256,128]{1,0:T(8,128)S(1)}, u32[]{:S(2)}, u32[]{:S(2)}) collective-permute-start(f32[256,128]{1,0:T(8,128)} %bitcast.73), channel_id=1, source_target_pairs={{16,0},{32,16},{48,32},{64,48},{80,64},{96,80},{112,96},{128,112},... | collective-permute-start | bytes 393224 | tf_op jit(solution)/shard_map/ppermute | solution.py:16
  401.0 8.4 collective-permute-start.10
  402.3 11.3 %collective-permute-start.11 = (f32[256,128]{1,0:T(8,128)}, f32[256,128]{1,0:T(8,128)}, u32[]{:S(2)}, u32[]{:S(2)}) collective-permute-start(f32[256,128]{1,0:T(8,128)} %bitcast.57), channel_id=1, source_target_pairs={{64,0},{80,16},{96,32},{112,48},{128,64},{144,80},{160,96},{176,11... | collective-permute-start | bytes 393224 | tf_op jit(solution)/shard_map/ppermute | solution.py:16
  403.6 11.3 %collective-permute-start.8 = (f32[256,128]{1,0:T(8,128)}, f32[256,128]{1,0:T(8,128)}, u32[]{:S(2)}, u32[]{:S(2)}) collective-permute-start(f32[256,128]{1,0:T(8,128)} %bitcast.54), channel_id=1, source_target_pairs={{16,0},{32,16},{48,32},{64,48},{80,64},{96,80},{112,96},{128,112},... | collective-permute-start | bytes 393224 | tf_op jit(solution)/shard_map/ppermute | solution.py:16
  404.9 11.3 %collective-permute-start.9 = (f32[256,128]{1,0:T(8,128)}, f32[256,128]{1,0:T(8,128)}, u32[]{:S(2)}, u32[]{:S(2)}) collective-permute-start(f32[256,128]{1,0:T(8,128)} %bitcast.55), channel_id=1, source_target_pairs={{32,0},{48,16},{64,32},{80,48},{96,64},{112,80},{128,96},{144,112}... | collective-permute-start | bytes 393224 | tf_op jit(solution)/shard_map/ppermute | solution.py:16
  406.5 2.9 copy-start.9
  406.5 7.1 copy-start.8
  406.5 8.4 copy-start.7
  406.5 10.8 %copy-start.1 = (bf16[5376,128]{1,0:T(8,128)(2,1)S(1)}, bf16[5376,128]{1,0:T(8,128)(2,1)}, u32[]{:S(2)}) copy-start(bf16[5376,128]{1,0:T(8,128)(2,1)} %all-gather.9.cloned.1.call-done) | copy-start | bytes 4128772
  409.4 10.3 %collective-permute-start.13 = (f32[256,128]{1,0:T(8,128)S(1)}, f32[256,128]{1,0:T(8,128)S(1)}, u32[]{:S(2)}, u32[]{:S(2)}) collective-permute-start(f32[256,128]{1,0:T(8,128)S(1)} %bitcast.356), channel_id=1, source_target_pairs={{32,0},{48,16},{64,32},{80,48},{96,64},{112,80},{128,96},{144,112}... | collective-permute-start | bytes 393224 | tf_op jit(solution)/shard_map/ppermute | solution.py:16
  413.6 7.4 collective-permute-start.14
  414.9 11.4 %collective-permute-start.15 = (f32[256,128]{1,0:T(8,128)S(1)}, f32[256,128]{1,0:T(8,128)S(1)}, u32[]{:S(2)}, u32[]{:S(2)}) collective-permute-start(f32[256,128]{1,0:T(8,128)S(1)} %bitcast.354), channel_id=1, source_target_pairs={{64,0},{80,16},{96,32},{112,48},{128,64},{144,80},{160,96},{176,11... | collective-permute-start | bytes 393224 | tf_op jit(solution)/shard_map/ppermute | solution.py:16
  417.4 9.0 copy-start.2
  429.7 291.3 %reduce-scatter.20.cloned.1.call-start = ((), (), s32[]{:S(2)}) async-start(), calls=%async_computation.14 | async-start | bytes 1462272
  434.5 353.8 %reduce-scatter.18.cloned.1.call-start = ((), (), s32[]{:S(2)}) async-start(), calls=%async_computation.13 | async-start | bytes 1462272
  439.2 418.2 %reduce-scatter.16.cloned.1.call-start = ((), (), s32[]{:S(2)}) async-start(), calls=%async_computation.12 | async-start | bytes 2924544
  446.4 480.4 %reduce-scatter.22.cloned.1.call-start = ((), (), s32[]{:S(2)}) async-start(), calls=%async_computation.15 | async-start | bytes 2924544
Sparse Core Ops, SparseCore 0:
  9.8 37.7 all-gather.8
  50.2 89.5 all-gather.6
  141.6 35.5 all-gather.10
  179.7 88.5 all-gather.14
  269.9 34.5 all-gather.16
  306.2 35.3 all-gather.12
  429.8 223.5 reduce-scatter.13
  656.5 64.4 reduce-scatter.19
  724.1 64.1 reduce-scatter.17
  791.2 66.1 reduce-scatter.15
  860.5 66.1 reduce-scatter.21
where the time goes:
time: 935 us; the launch traced here: 933 us
  waiting for transfers between devices  793 us (85%)
  starting transfers between devices  37.1 us (4%)
  matrix products  35.7 us (4%)
  local copies, waits for them, and re-layouts  31.4 us (3%)
  other arithmetic  22.1 us (2%)
  between operations  14.4 us (2%)
    unnamed x15, waiting for transfers between devices  275 us
    reduce_scatter x1, waiting for transfers between devices, shards(): lax.psum_scatter(token_term, 'tp', scatter_dimension=1, tiled=True)  201 us
    all_gather x1, waiting for transfers between devices, shards(): lax.all_gather(tokens, 'tp', axis=1, tiled=True)  92.1 us
    all_gather x1, waiting for transfers between devices, shards(): lax.all_gather(cotangent, 'tp', axis=1, tiled=True)  87.6 us
    ppermute x16, starting transfers between devices, from_behind(): return lax.ppermute(block, axis, route)  36.6 us
    all_gather x1, waiting for transfers between devices, shards(): lax.all_gather(w_out, 'seq', axis=1, tiled=True)  36.3 us
    all_gather x1, waiting for transfers between devices, shards(): lax.all_gather(w_key, 'seq', axis=0, tiled=True)  35 us
    all_gather x1, waiting for transfers between devices, shards(): lax.all_gather(w_value, 'seq', axis=0, tiled=True)  33.5 us
  transfers between devices with their start and end apart: 27, of which 15 were waited for; matrix products, arithmetic and copies ran while one was open for 8% of the time, Pallas kernels for 0%

commit v1 on v0

--- a/solution.py
+++ b/solution.py
@@ -101,7 +101,9 @@
     reach = WIN // tok_rows
     full_tokens, full_cot = (
         lax.all_gather(tokens, "tp", axis=1, tiled=True),
-        lax.all_gather(cotangent, "tp", axis=1, tiled=True),
+        jnp.concatenate(
+            lax.all_to_all(jnp.stack([cotangent] * lax.axis_size("tp")), "tp", 0, 0), axis=1
+        ),
     )
     query_full, key_full, value_full = (
         lax.all_gather(w_query, "seq", axis=0, tiled=True),

time: 935 us -> 855 us (0.914)
  waiting for transfers between devices: 793 us -> 696 us
  starting transfers between devices: 37.1 us -> 48.4 us
    all_gather x1 -> x0, waiting for transfers between devices: 87.6 us -> none  [shards(): lax.all_gather(cotangent, 'tp', axis=1, tiled=True)]
    all_gather x1, waiting for transfers between devices: 35 us -> 22.3 us  [shards(): lax.all_gather(w_key, 'seq', axis=0, tiled=True)]
    all_to_all x0 -> x1, starting transfers between devices: none -> 11.3 us  [shards(): lax.all_to_all(jnp.stack([cotangent] * lax.axis_size('tp')), 'tp', 0, 0)]
    unnamed x15 -> x14, waiting for transfers between devices: 275 us -> 275 us
  transfers between devices with their start and end apart: 27 -> 27, of which waited for: 15 -> 14; matrix products, arithmetic and copies ran while one was open for 8% -> 9% of each run, Pallas kernels for 0% -> 0%
where the time goes in v1:
time: 855 us; the launch traced here: 853 us
  waiting for transfers between devices  696 us (81%)
  starting transfers between devices  48.4 us (6%)
  matrix products  37.2 us (4%)
  local copies, waits for them, and re-layouts  35.9 us (4%)
  other arithmetic  21.4 us (3%)
  between operations  14.7 us (2%)
    unnamed x14, waiting for transfers between devices  275 us
    reduce_scatter x1, waiting for transfers between devices, shards(): lax.psum_scatter(token_term, 'tp', scatter_dimension=1, tiled=True)  198 us
    all_gather x1, waiting for transfers between devices, shards(): lax.all_gather(tokens, 'tp', axis=1, tiled=True)  101 us
    ppermute x16, starting transfers between devices, from_behind(): return lax.ppermute(block, axis, route)  36.6 us
    all_gather x1, waiting for transfers between devices, shards(): lax.all_gather(w_out, 'seq', axis=1, tiled=True)  34.8 us
    all_gather x1, waiting for transfers between devices, shards(): lax.all_gather(w_value, 'seq', axis=0, tiled=True)  33.5 us
    all_gather x1, waiting for transfers between devices, shards(): lax.all_gather(w_key, 'seq', axis=0, tiled=True)  22.3 us
    all_gather x1, waiting for transfers between devices, shards(): lax.all_gather(w_query, 'seq', axis=0, tiled=True)  20.5 us
  transfers between devices with their start and end apart: 27, of which 14 were waited for; matrix products, arithmetic and copies ran while one was open for 9% of the time, Pallas kernels for 0%

profile of v1, /device:TPU:32, one launch (start us, length us, event | category | flops | bytes accessed | tf_op | source)
XLA Modules:
  0.0 853.4 jit_solution(15889752976756701104)
XLA Ops:
  10.0 2.7 stack.2
  12.7 11.3 %all-to-all-start = ((bf16[16,256,336]{1,2,0:T(8,128)(2,1)}), bf16[16,256,336]{1,2,0:T(8,128)(2,1)}, u32[]{:S(2)}, u32[]{:S(2)}) async-start(bf16[16,256,336]{1,2,0:T(8,128)(2,1)} %stack.2), calls=%async_computation | async-start | bytes 5505024 | tf_op jit(solution)/shard_map/all_to_all | solution.py:105
  25.4 22.3 %all-gather.8.cloned.1.call-done = bf16[5376,128]{1,0:T(8,128)(2,1)} async-done(((bf16[336,128]{1,0:T(8,128)(2,1)}), bf16[5376,128]{1,0:T(8,128)(2,1)}) %all-gather.8.cloned.1.call-update) | async-done | bytes 1376272 | tf_op jit(solution)/shard_map/all_gather | solution.py:110
  47.8 100.8 %all-gather.6.cloned.1.call-done = bf16[256,5376]{0,1:T(8,128)(2,1)} async-done(((bf16[256,336]{0,1:T(8,128)(2,1)}), bf16[256,5376]{0,1:T(8,128)(2,1)}) %all-gather.6.cloned.1.call-update) | async-done | bytes 2752528 | tf_op jit(solution)/shard_map/all_gather | solution.py:103
  148.6 3.2 convolution_convert_fusion.7
  151.8 5.5 collective-permute-start
  157.3 1.9 collective-permute-start.1
  159.2 3.1 collective-permute-start.2
  162.3 3.2 collective-permute-start.3
  165.5 20.5 %all-gather.10.cloned.1.call-done = bf16[5376,256]{1,0:T(8,128)(2,1)} async-done(((bf16[336,256]{1,0:T(8,128)(2,1)}), bf16[5376,256]{1,0:T(8,128)(2,1)}) %all-gather.10.cloned.1.call-update) | async-done | bytes 2752528 | tf_op jit(solution)/shard_map/all_gather | solution.py:109
  186.1 3.4 convolution_convert_fusion.5
  189.4 34.8 %all-gather.14.cloned.1.call-done = bf16[256,5376]{0,1:T(8,128)(2,1)} async-done(((bf16[256,336]{0,1:T(8,128)(2,1)}), bf16[256,5376]{0,1:T(8,128)(2,1)}) %all-gather.14.cloned.1.call-update) | async-done | bytes 2752528 | tf_op jit(solution)/shard_map/all_gather | solution.py:113
  224.3 3.5 convolution_convert_fusion.4
  227.8 33.5 %all-gather.12.cloned.1.call-done = bf16[5376,128]{1,0:T(8,128)(2,1)} async-done(((bf16[336,128]{1,0:T(8,128)(2,1)}), bf16[5376,128]{1,0:T(8,128)(2,1)}) %all-gather.12.cloned.1.call-update) | async-done | bytes 1376272 | tf_op jit(solution)/shard_map/all_gather | solution.py:111
  261.3 2.3 convolution_convert_fusion.6
  264.3 1.0 reshape.840
  265.3 1.6 reshape.813
  266.9 1.7 copy.87
  268.6 1.7 copy.98
  270.3 4.0 collective-permute-start.4
  275.1 2.0 collective-permute-start.5
  277.9 3.5 collective-permute-start.6
  281.4 3.0 collective-permute-start.7
  288.0 1.4 fusion.79
  289.9 1.8 convolution_bitcast_fusion.1
  293.6 1.5 fusion.11
  295.5 2.7 copy.100
  300.1 0.9 fusion.53
  301.1 0.9 fusion.51
  303.9 0.9 fusion.45
  304.8 0.9 fusion.43
  305.8 1.7 fusion.41
  307.5 1.3 collective-permute-start.12
  308.8 2.7 copy.89
  313.4 0.9 fusion.66
  319.0 1.7 fusion.54
  320.8 1.3 collective-permute-start.10
  322.0 1.3 collective-permute-start.11
  323.3 1.3 collective-permute-start.8
  324.6 1.5 collective-permute-start.9
  326.3 2.8 fusion.39
  329.1 1.3 collective-permute-start.13
  330.4 2.9 collective-permute-done.11
  333.4 1.3 collective-permute-start.14
  334.7 1.3 collective-permute-start.15
  336.0 1.1 fusion.74
  338.0 1.4 collective-permute-done.13
  339.4 1.4 collective-permute-done.14
  340.8 5.3 collective-permute-done.15
  346.1 3.3 convolution_add_fusion
  349.5 2.2 fusion.3
  351.7 2.5 copy.132
  354.3 2.2 fusion.2
  356.4 2.5 copy.130
  359.2 4.3 fusion.1
  363.5 4.7 copy.134
  368.2 2.6 fusion
  370.8 4.5 copy.128
  375.3 198.0 %reduce-scatter.14.cloned.1.call-done = f32[256,336]{0,1:T(8,128)} async-done(((f32[256,5376]{0,1:T(8,128)}), f32[256,336]{0,1:T(8,128)}) %reduce-scatter.14.cloned.1.call-update) | async-done | bytes 344080 | tf_op jit(solution)/shard_map/reduce_scatter | solution.py:156
  573.3 1.7 convert_element_type.114
  575.0 65.8 %reduce-scatter.20.cloned.1.call-done = bf16[336,128]{1,0:T(8,128)(2,1)} async-done(((bf16[5376,128]{1,0:T(8,128)(2,1)}), bf16[336,128]{1,0:T(8,128)(2,1)}) %reduce-scatter.20.cloned.1.call-update) | async-done | bytes 86032
  640.8 67.3 %reduce-scatter.18.cloned.1.call-done = bf16[336,128]{1,0:T(8,128)(2,1)} async-done(((bf16[5376,128]{1,0:T(8,128)(2,1)}), bf16[336,128]{1,0:T(8,128)(2,1)}) %reduce-scatter.18.cloned.1.call-update) | async-done | bytes 86032
  708.1 69.3 %reduce-scatter.22.cloned.1.call-done = bf16[336,256]{1,0:T(8,128)(2,1)} async-done(((bf16[5376,256]{1,0:T(8,128)(2,1)}), bf16[336,256]{1,0:T(8,128)(2,1)}) %reduce-scatter.22.cloned.1.call-update) | async-done | bytes 172048
  777.4 69.2 %reduce-scatter.16.cloned.1.call-done = bf16[336,256]{1,0:T(8,128)(2,1)} async-done(((bf16[5376,256]{1,0:T(8,128)(2,1)}), bf16[336,256]{1,0:T(8,128)(2,1)}) %reduce-scatter.16.cloned.1.call-update) | async-done | bytes 172048
  (104 shorter events, 24.5 us)
Async XLA Ops:
  7.2 40.6 %all-gather.8.cloned.1.call-start = ((), (), s32[]{:S(2)}) async-start(), calls=%async_computation.7 | async-start | bytes 1462272 | tf_op jit(solution)/shard_map/all_gather | solution.py:110
  7.9 140.7 %all-gather.6.cloned.1.call-start = ((), (), s32[]{:S(2)}) async-start(), calls=%async_computation.6 | async-start | bytes 2924544 | tf_op jit(solution)/shard_map/all_gather | solution.py:103
  8.6 177.4 %all-gather.10.cloned.1.call-start = ((), (), s32[]{:S(2)}) async-start(), calls=%async_computation.8 | async-start | bytes 2924544 | tf_op jit(solution)/shard_map/all_gather | solution.py:109
  9.4 214.9 %all-gather.14.cloned.1.call-start = ((), (), s32[]{:S(2)}) async-start(), calls=%async_computation.10 | async-start | bytes 2924544 | tf_op jit(solution)/shard_map/all_gather | solution.py:113
  12.7 12.0 %copy-start.10 = (s32[2,9]{1,0:T(2,128)S(1)}, s32[2,9]{1,0:T(2,128)}, u32[]{:S(2)}) copy-start(s32[2,9]{1,0:T(2,128)} %param.49) | copy-start | bytes 220
  12.7 176.8 %all-to-all-start = ((bf16[16,256,336]{1,2,0:T(8,128)(2,1)}), bf16[16,256,336]{1,2,0:T(8,128)(2,1)}, u32[]{:S(2)}, u32[]{:S(2)}) async-start(bf16[16,256,336]{1,2,0:T(8,128)(2,1)} %stack.2), calls=%async_computation | async-start | bytes 5505024 | tf_op jit(solution)/shard_map/all_to_all | solution.py:105
  24.0 237.3 %all-gather.12.cloned.1.call-start = ((), (), s32[]{:S(2)}) async-start(), calls=%async_computation.9 | async-start | bytes 1462272 | tf_op jit(solution)/shard_map/all_gather | solution.py:111
  24.6 548.7 %reduce-scatter.14.cloned.1.call-start = ((), (), s32[]{:S(2)}) async-start(), calls=%async_computation.11 | async-start | bytes 5849088 | tf_op jit(solution)/shard_map/reduce_scatter | solution.py:156
  148.6 37.5 %copy-start = (bf16[256,5376]{0,1:T(8,128)(2,1)S(1)}, bf16[256,5376]{0,1:T(8,128)(2,1)}, u32[]{:S(2)}) copy-start(bf16[256,5376]{0,1:T(8,128)(2,1)} %all-gather.6.cloned.1.call-done) | copy-start | bytes 8257540
  151.8 123.3 %collective-permute-start = (bf16[256,128]{1,0:T(8,128)(2,1)S(1)}, bf16[256,128]{1,0:T(8,128)(2,1)}, u32[]{:S(2)}, u32[]{:S(2)}) collective-permute-start(bf16[256,128]{1,0:T(8,128)(2,1)S(1)} %convolution_convert_fusion.7), channel_id=1, source_target_pairs={{0,64},{16,80},{32,96},{48,112},{64,128},{80,144},{96,160},{112,17... | collective-permute-start | bytes 196616 | tf_op jit(solution)/shard_map/ppermute | solution.py:16
  157.3 120.6 %collective-permute-start.1 = (bf16[256,128]{1,0:T(8,128)(2,1)S(1)}, bf16[256,128]{1,0:T(8,128)(2,1)}, u32[]{:S(2)}, u32[]{:S(2)}) collective-permute-start(bf16[256,128]{1,0:T(8,128)(2,1)S(1)} %convolution_convert_fusion.7), channel_id=1, source_target_pairs={{0,48},{16,64},{32,80},{48,96},{64,112},{80,128},{96,144},{112,160... | collective-permute-start | bytes 196616 | tf_op jit(solution)/shard_map/ppermute | solution.py:16
  159.2 122.2 %collective-permute-start.2 = (bf16[256,128]{1,0:T(8,128)(2,1)S(1)}, bf16[256,128]{1,0:T(8,128)(2,1)}, u32[]{:S(2)}, u32[]{:S(2)}) collective-permute-start(bf16[256,128]{1,0:T(8,128)(2,1)S(1)} %convolution_convert_fusion.7), channel_id=1, source_target_pairs={{0,32},{16,48},{32,64},{48,80},{64,96},{80,112},{96,128},{112,144}... | collective-permute-start | bytes 196616 | tf_op jit(solution)/shard_map/ppermute | solution.py:16
  162.3 122.1 %collective-permute-start.3 = (bf16[256,128]{1,0:T(8,128)(2,1)S(1)}, bf16[256,128]{1,0:T(8,128)(2,1)}, u32[]{:S(2)}, u32[]{:S(2)}) collective-permute-start(bf16[256,128]{1,0:T(8,128)(2,1)S(1)} %convolution_convert_fusion.7), channel_id=1, source_target_pairs={{0,16},{16,32},{32,48},{48,64},{64,80},{80,96},{96,112},{112,128},... | collective-permute-start | bytes 196616 | tf_op jit(solution)/shard_map/ppermute | solution.py:16
  227.8 35.8 %copy-start.4 = (bf16[256,256]{1,0:T(8,128)(2,1)}, bf16[256,256]{1,0:T(8,128)(2,1)S(1)}, u32[]{:S(2)}) copy-start(bf16[256,256]{1,0:T(8,128)(2,1)S(1)} %convolution_convert_fusion.4) | copy-start | bytes 393220
  270.3 21.4 %collective-permute-start.4 = (bf16[256,128]{1,0:T(8,128)(2,1)S(1)}, bf16[256,128]{1,0:T(8,128)(2,1)S(1)}, u32[]{:S(2)}, u32[]{:S(2)}) collective-permute-start(bf16[256,128]{1,0:T(8,128)(2,1)S(1)} %convolution_convert_fusion.6), channel_id=1, source_target_pairs={{0,64},{16,80},{32,96},{48,112},{64,128},{80,144},{96,160},{112,17... | collective-permute-start | bytes 196616 | tf_op jit(solution)/shard_map/ppermute | solution.py:16
  275.1 16.6 %collective-permute-start.5 = (bf16[256,128]{1,0:T(8,128)(2,1)S(1)}, bf16[256,128]{1,0:T(8,128)(2,1)S(1)}, u32[]{:S(2)}, u32[]{:S(2)}) collective-permute-start(bf16[256,128]{1,0:T(8,128)(2,1)S(1)} %convolution_convert_fusion.6), channel_id=1, source_target_pairs={{0,48},{16,64},{32,80},{48,96},{64,112},{80,128},{96,144},{112,160... | collective-permute-start | bytes 196616 | tf_op jit(solution)/shard_map/ppermute | solution.py:16
  277.9 13.8 %collective-permute-start.6 = (bf16[256,128]{1,0:T(8,128)(2,1)S(1)}, bf16[256,128]{1,0:T(8,128)(2,1)S(1)}, u32[]{:S(2)}, u32[]{:S(2)}) collective-permute-start(bf16[256,128]{1,0:T(8,128)(2,1)S(1)} %convolution_convert_fusion.6), channel_id=1, source_target_pairs={{0,32},{16,48},{32,64},{48,80},{64,96},{80,112},{96,128},{112,144}... | collective-permute-start | bytes 196616 | tf_op jit(solution)/shard_map/ppermute | solution.py:16
  281.4 10.3 %collective-permute-start.7 = (bf16[256,128]{1,0:T(8,128)(2,1)S(1)}, bf16[256,128]{1,0:T(8,128)(2,1)S(1)}, u32[]{:S(2)}, u32[]{:S(2)}) collective-permute-start(bf16[256,128]{1,0:T(8,128)(2,1)S(1)} %convolution_convert_fusion.6), channel_id=1, source_target_pairs={{0,16},{16,32},{32,48},{48,64},{64,80},{80,96},{96,112},{112,128},... | collective-permute-start | bytes 196616 | tf_op jit(solution)/shard_map/ppermute | solution.py:16
  288.0 1.9 copy-start.6
  289.9 2.0 copy-start.5
  292.7 0.9 copy-start.3
  307.5 30.5 %collective-permute-start.12 = (f32[256,128]{1,0:T(8,128)}, f32[256,128]{1,0:T(8,128)S(1)}, u32[]{:S(2)}, u32[]{:S(2)}) collective-permute-start(f32[256,128]{1,0:T(8,128)} %bitcast.75), channel_id=1, source_target_pairs={{16,0},{32,16},{48,32},{64,48},{80,64},{96,80},{112,96},{128,112},... | collective-permute-start | bytes 393224 | tf_op jit(solution)/shard_map/ppermute | solution.py:16
  320.8 8.4 collective-permute-start.10
  322.0 11.3 %collective-permute-start.11 = (f32[256,128]{1,0:T(8,128)}, f32[256,128]{1,0:T(8,128)}, u32[]{:S(2)}, u32[]{:S(2)}) collective-permute-start(f32[256,128]{1,0:T(8,128)} %bitcast.59), channel_id=1, source_target_pairs={{64,0},{80,16},{96,32},{112,48},{128,64},{144,80},{160,96},{176,11... | collective-permute-start | bytes 393224 | tf_op jit(solution)/shard_map/ppermute | solution.py:16
  323.3 11.3 %collective-permute-start.8 = (f32[256,128]{1,0:T(8,128)}, f32[256,128]{1,0:T(8,128)}, u32[]{:S(2)}, u32[]{:S(2)}) collective-permute-start(f32[256,128]{1,0:T(8,128)} %bitcast.56), channel_id=1, source_target_pairs={{16,0},{32,16},{48,32},{64,48},{80,64},{96,80},{112,96},{128,112},... | collective-permute-start | bytes 393224 | tf_op jit(solution)/shard_map/ppermute | solution.py:16
  324.6 11.3 %collective-permute-start.9 = (f32[256,128]{1,0:T(8,128)}, f32[256,128]{1,0:T(8,128)}, u32[]{:S(2)}, u32[]{:S(2)}) collective-permute-start(f32[256,128]{1,0:T(8,128)} %bitcast.57), channel_id=1, source_target_pairs={{32,0},{48,16},{64,32},{80,48},{96,64},{112,80},{128,96},{144,112}... | collective-permute-start | bytes 393224 | tf_op jit(solution)/shard_map/ppermute | solution.py:16
  326.3 2.9 copy-start.9
  326.3 7.1 copy-start.8
  326.3 8.4 copy-start.7
  326.3 10.8 %copy-start.1 = (bf16[5376,128]{1,0:T(8,128)(2,1)S(1)}, bf16[5376,128]{1,0:T(8,128)(2,1)}, u32[]{:S(2)}) copy-start(bf16[5376,128]{1,0:T(8,128)(2,1)} %all-gather.8.cloned.1.call-done) | copy-start | bytes 4128772
  329.1 10.2 %collective-permute-start.13 = (f32[256,128]{1,0:T(8,128)S(1)}, f32[256,128]{1,0:T(8,128)S(1)}, u32[]{:S(2)}, u32[]{:S(2)}) collective-permute-start(f32[256,128]{1,0:T(8,128)S(1)} %bitcast.359), channel_id=1, source_target_pairs={{32,0},{48,16},{64,32},{80,48},{96,64},{112,80},{128,96},{144,112}... | collective-permute-start | bytes 393224 | tf_op jit(solution)/shard_map/ppermute | solution.py:16
  333.4 7.4 collective-permute-start.14
  334.7 11.4 %collective-permute-start.15 = (f32[256,128]{1,0:T(8,128)S(1)}, f32[256,128]{1,0:T(8,128)S(1)}, u32[]{:S(2)}, u32[]{:S(2)}) collective-permute-start(f32[256,128]{1,0:T(8,128)S(1)} %bitcast.357), channel_id=1, source_target_pairs={{64,0},{80,16},{96,32},{112,48},{128,64},{144,80},{160,96},{176,11... | collective-permute-start | bytes 393224 | tf_op jit(solution)/shard_map/ppermute | solution.py:16
  337.1 9.0 %copy-start.2 = (bf16[5376,128]{1,0:T(8,128)(2,1)S(1)}, bf16[5376,128]{1,0:T(8,128)(2,1)}, u32[]{:S(2)}) copy-start(bf16[5376,128]{1,0:T(8,128)(2,1)} %all-gather.12.cloned.1.call-done) | copy-start | bytes 4128772
  349.4 291.4 %reduce-scatter.20.cloned.1.call-start = ((), (), s32[]{:S(2)}) async-start(), calls=%async_computation.14 | async-start | bytes 1462272
  354.2 353.9 %reduce-scatter.18.cloned.1.call-start = ((), (), s32[]{:S(2)}) async-start(), calls=%async_computation.13 | async-start | bytes 1462272
  359.0 418.4 %reduce-scatter.22.cloned.1.call-start = ((), (), s32[]{:S(2)}) async-start(), calls=%async_computation.15 | async-start | bytes 2924544
  368.1 478.4 %reduce-scatter.16.cloned.1.call-start = ((), (), s32[]{:S(2)}) async-start(), calls=%async_computation.12 | async-start | bytes 2924544
Sparse Core Ops, SparseCore 0:
  9.8 37.8 all-gather.7
  50.3 98.1 all-gather.5
  150.4 35.6 all-gather.9
  187.8 36.4 all-gather.13
  226.0 35.3 all-gather.11
  349.6 223.7 reduce-scatter.13
  576.4 64.3 reduce-scatter.19
  643.9 64.1 reduce-scatter.17
  711.2 66.1 reduce-scatter.21
  780.4 66.1 reduce-scatter.15
